TPU v7x, 32 devices: a whole 2x2x4 slice. The times are simulated.
32 devices in a mesh: blk: 8 (over y, x, core), head: 4 (over z).
Axes of the slice: x: 2, y: 2, z: 4, core: 2. Of those that a mesh axis runs over, the one named last changes fastest.
Arguments:
- queries: bfloat16 [6144, 512], P('blk', 'head'), may hold values from -56 to 56
- key_states: bfloat16 [6144, 512], P('blk', 'head'), may hold values from -4 to 4
- value_states: bfloat16 [6144, 512], P('blk', 'head'), may hold values from -6 to 6
- out_grad: bfloat16 [6144, 512], P('blk', 'head'), may hold values from -6 to 6
- out_weight: bfloat16 [512, 512], P('head'), may hold values from -0.25 to 0.25
- counts: int32 [8], replicated, may hold values from 192 to 768, as said below
- patch_links: int32 [8, 3], replicated, may hold values 0 or 1
Outputs:
- attended: bfloat16 [6144, 512], P('blk', 'head')
- query_grad: bfloat16 [6144, 512], P('blk', 'head')
- key_grad: bfloat16 [6144, 512], P('blk', 'head')
- value_grad: bfloat16 [6144, 512], P('blk', 'head')
Inputs may be any that keep to these rules, and one draw needn't show every extreme that they name: `counts`: some patch has all 768 points live.
All inputs are finite; a program needn't handle non-finite values.
Results may differ from a plain program's by a relative error of at most 0.02.
Values may be sent and summed in bfloat16 or wider, within the bound.
A program may use at most 64 MiB of HBM per device.

v0:
```python
import math

import jax
import jax.numpy as jnp
from jax import lax
from jax.sharding import PartitionSpec as P

HD = 64


MASKED = -1e30


def passed_along(value, axis, by):
    size = lax.axis_size(axis)
    return lax.ppermute(value, axis, [(i, (i + by) % size) for i in range(size)])


def lookup(stacked, wanted):
    ordinal = jnp.arange(stacked.shape[0], dtype=jnp.int32)
    return jnp.sum(jnp.where(ordinal == wanted, stacked, 0))


def live_keys(counts, patch_links, cycle_index, cycle_size, points):
    distances = (0, -1, 1, cycle_size // 2)
    position = jnp.arange(points, dtype=jnp.int32)
    masks = []
    for slot_index in range(4):
        owner_block = (cycle_index + distances[slot_index]) % cycle_size
        usable = position < lookup(counts, owner_block)
        if slot_index > 0:
            linked = lookup(patch_links[:, slot_index - 1], cycle_index) == 1
            usable = jnp.logical_and(usable, linked)
        masks.append(usable)
    return jnp.concatenate(masks)


def attention_weights(query_rows, key_rows, key_live, scaling):
    scores = (
        lax.dot_general(
            query_rows, key_rows, (((1,), (1,)), ((), ())), preferred_element_type=jnp.float32
        )
        * scaling
    )
    scores = jnp.where(key_live[None, :], scores, MASKED)
    maximum = jnp.max(scores, axis=1, keepdims=True)
    powers = jnp.exp(scores - maximum)
    total = jnp.sum(powers, axis=1, keepdims=True)
    return (powers / total, maximum, total)


def fetch_blocks(key_states, value_states, cycle_size):
    key_pieces = [key_states]
    value_pieces = [value_states]
    for distance in (1, -1, cycle_size // 2):
        arrived = passed_along((key_states, value_states), "blk", distance)
        key_pieces.append(arrived[0])
        value_pieces.append(arrived[1])
    return (jnp.concatenate(key_pieces), jnp.concatenate(value_pieces))


def fetch_again(key_states, value_states, cycle_size):
    key_pieces = [key_states]
    value_pieces = [value_states]
    for distance in (1, -1, cycle_size // 2):
        arrived = passed_along((key_states, value_states), "blk", distance)
        key_pieces.append(arrived[0])
        value_pieces.append(arrived[1])
    return (jnp.concatenate(key_pieces), jnp.concatenate(value_pieces))


def head_forward(query_head, key_rows, value_rows, key_live, query_live, row_block, scaling):
    points, head_size = query_head.shape
    blocks = points // row_block

    def one_block(inputs):
        query_rows, live_rows = inputs
        weights = attention_weights(query_rows, key_rows, key_live, scaling)[0]
        rounded = (weights * live_rows[:, None]).astype(jnp.bfloat16)
        return jnp.dot(rounded, value_rows, preferred_element_type=jnp.float32)

    result = lax.map(
        one_block,
        (query_head.reshape(blocks, row_block, head_size), query_live.reshape(blocks, row_block)),
    )
    return result.reshape(points, head_size)


def head_backward(
    query_head,
    key_rows,
    value_rows,
    key_live,
    query_live,
    grad_head,
    attended_head,
    row_block,
    scaling,
):
    points, head_size = query_head.shape
    blocks = points // row_block

    def one_block(running, inputs):
        key_sum, value_sum = running
        query_rows, live_rows, grad_rows, attended_rows = inputs
        weights, maximum, total = attention_weights(query_rows, key_rows, key_live, scaling)
        masked_weights = weights * live_rows[:, None]
        rounded = masked_weights.astype(jnp.bfloat16)
        weight_grad = lax.dot_general(
            grad_rows, value_rows, (((1,), (1,)), ((), ())), preferred_element_type=jnp.float32
        )
        row_inner = jnp.sum(grad_rows.astype(jnp.float32) * attended_rows, axis=1, keepdims=True)
        score_grad = (masked_weights * (weight_grad - row_inner)).astype(jnp.bfloat16)
        query_part = (
            jnp.dot(score_grad, key_rows, preferred_element_type=jnp.float32) * scaling
        ).astype(jnp.bfloat16)
        key_sum = (
            key_sum
            + lax.dot_general(
                score_grad, query_rows, (((0,), (0,)), ((), ())), preferred_element_type=jnp.float32
            )
            * scaling
        )
        value_sum = value_sum + lax.dot_general(
            rounded, grad_rows, (((0,), (0,)), ((), ())), preferred_element_type=jnp.float32
        )
        return ((key_sum, value_sum), (query_part, maximum[:, 0], total[:, 0], row_inner[:, 0]))

    zeros_start = jnp.zeros((key_rows.shape[0], head_size), jnp.float32)
    inputs = (
        query_head.reshape(blocks, row_block, head_size),
        query_live.reshape(blocks, row_block),
        grad_head.reshape(blocks, row_block, head_size),
        attended_head.reshape(blocks, row_block, head_size),
    )
    sums, outputs = lax.scan(one_block, (zeros_start, zeros_start), inputs)
    return (
        sums[0],
        sums[1],
        outputs[0].reshape(points, head_size),
        outputs[1].reshape(points),
        outputs[2].reshape(points),
        outputs[3].reshape(points),
    )


def body(queries, key_states, value_states, out_grad, out_weight, counts, patch_links):
    cycle_size = lax.axis_size("blk")
    cycle_index = lax.axis_index("blk")
    points, features = queries.shape
    local_heads = features // HD
    scaling = 1.0 / math.sqrt(HD)
    row_block = math.gcd(points, 256)
    position = jnp.arange(points, dtype=jnp.int32)
    key_live = live_keys(counts, patch_links, cycle_index, cycle_size, points)
    query_live = (position < lookup(counts, cycle_index)).astype(jnp.float32)
    seen_keys, seen_values = fetch_blocks(key_states, value_states, cycle_size)
    attended_heads = []
    for head_number in range(local_heads):
        first_column = head_number * HD
        attended_heads.append(
            head_forward(
                queries[:, first_column : first_column + HD],
                seen_keys[:, first_column : first_column + HD],
                seen_values[:, first_column : first_column + HD],
                key_live,
                query_live,
                row_block,
                scaling,
            )
        )
    attended_f = jnp.concatenate(attended_heads, axis=1)
    features_rounded = attended_f.astype(jnp.bfloat16)
    partial_out = jnp.dot(features_rounded, out_weight, preferred_element_type=jnp.float32)
    attended = lax.psum_scatter(
        partial_out.astype(jnp.bfloat16), "head", scatter_dimension=1, tiled=True
    )
    grad_features = lax.dot_general(
        lax.all_gather(out_grad, "head", axis=1, tiled=True),
        out_weight,
        (((1,), (1,)), ((), ())),
        preferred_element_type=jnp.float32,
    ).astype(jnp.bfloat16)
    back_keys, back_values = fetch_again(key_states, value_states, cycle_size)
    key_columns = []
    value_columns = []
    query_columns = []
    maxima_rows = []
    totals_rows = []
    inner_rows = []
    for head_number in range(local_heads):
        first_column = head_number * HD
        key_sum, value_sum, query_part, maxima, totals, inner = head_backward(
            queries[:, first_column : first_column + HD],
            back_keys[:, first_column : first_column + HD],
            back_values[:, first_column : first_column + HD],
            key_live,
            query_live,
            grad_features[:, first_column : first_column + HD],
            attended_f[:, first_column : first_column + HD],
            row_block,
            scaling,
        )
        key_columns.append(key_sum)
        value_columns.append(value_sum)
        query_columns.append(query_part)
        maxima_rows.append(maxima)
        totals_rows.append(totals)
        inner_rows.append(inner)
    key_terms = jnp.concatenate(key_columns, axis=1)
    value_terms = jnp.concatenate(value_columns, axis=1)
    query_grad = jnp.concatenate(query_columns, axis=1)
    key_total = key_terms[:points]
    value_total = value_terms[:points]
    returns = (-1, 1, cycle_size // 2)
    for slot_index in range(3):
        lower = (slot_index + 1) * points
        arrived = (
            passed_along(
                key_terms[lower : lower + points].astype(jnp.bfloat16), "blk", returns[slot_index]
            ).astype(jnp.float32),
            passed_along(
                value_terms[lower : lower + points].astype(jnp.bfloat16), "blk", returns[slot_index]
            ).astype(jnp.float32),
        )
        key_total = key_total + arrived[0]
        value_total = value_total + arrived[1]
    return (attended, query_grad, key_total.astype(jnp.bfloat16), value_total.astype(jnp.bfloat16))


def solution(mesh):
    return jax.shard_map(
        body,
        mesh=mesh,
        in_specs=(
            P("blk", "head"),
            P("blk", "head"),
            P("blk", "head"),
            P("blk", "head"),
            P("head", None),
            P(),
            P(),
        ),
        out_specs=(P("blk", "head"), P("blk", "head"), P("blk", "head"), P("blk", "head")),
        check_vma=False,
    )
```

profile of v0, /device:TPU:0, one launch (start us, length us, event | category | flops | bytes accessed | tf_op | source)
XLA Modules:
  0.0 202.2 jit_solution(14004379595422837972)
XLA Ops:
  7.8 2.9 %collective-permute-start.1 = (bf16[768,128]{1,0:T(8,128)(2,1)}, bf16[768,128]{1,0:T(8,128)(2,1)S(1)}, u32[]{:S(2)}, u32[]{:S(2)}) collective-permute-start(bf16[768,128]{1,0:T(8,128)(2,1)} %param.16), channel_id=1, source_target_pairs={{0,28},{4,0},{8,4},{12,8},{16,12},{20,16},{24,20},{28,24},{1,29},{... | collective-permute-start | bytes 589832 | tf_op jit(solution)/shard_map/ppermute | solution.py:16
  10.7 2.2 %collective-permute-start.2 = (bf16[768,128]{1,0:T(8,128)(2,1)}, bf16[768,128]{1,0:T(8,128)(2,1)S(1)}, u32[]{:S(2)}, u32[]{:S(2)}) collective-permute-start(bf16[768,128]{1,0:T(8,128)(2,1)} %param.16), channel_id=1, source_target_pairs={{0,16},{4,20},{8,24},{12,28},{16,0},{20,4},{24,8},{28,12},{1,17},{... | collective-permute-start | bytes 589832 | tf_op jit(solution)/shard_map/ppermute | solution.py:16
  12.9 2.6 %collective-permute-start.4 = (bf16[768,128]{1,0:T(8,128)(2,1)}, bf16[768,128]{1,0:T(8,128)(2,1)}, u32[]{:S(2)}, u32[]{:S(2)}) collective-permute-start(bf16[768,128]{1,0:T(8,128)(2,1)} %param.17), channel_id=1, source_target_pairs={{0,28},{4,0},{8,4},{12,8},{16,12},{20,16},{24,20},{28,24},{1,29},{... | collective-permute-start | bytes 589832 | tf_op jit(solution)/shard_map/ppermute | solution.py:16
  24.1 18.4 %all_gather.3 = bf16[768,512]{1,0:T(8,128)(2,1)S(1)} all-gather(bf16[768,128]{1,0:T(8,128)(2,1)} %param.18), channel_id=1, replica_groups=mesh['blk'=8,'head'=4] {'head'}, dimensions={1}, use_global_device_ids=true | all-gather | bytes 983040 | tf_op jit(solution)/shard_map/all_gather | solution.py:179
  53.6 6.9 %while.50 = (s32[]{:T(128)}, f32[3,256,64]{1,2,0:T(8,128)S(1)}, pred[3072]{0:T(1024)(128)(4,1)S(1)}, bf16[3,256,64]{2,1,0:T(8,128)(2,1)S(1)}, bf16[3072,64]{1,0:...) while((s32[]{:T(128)}, f32[3,256,64]{1,2,0:T(8,128)S(1)}, ...), condition=%wide.region_11.12_spmd, body=%wide.region_8.11_spmd.sunk | while | flops 208403968 | bytes 11152481 | solution.py:82
  61.8 42.2 %while.52 = (s32[]{:T(128)}, f32[3072,64]{0,1:T(8,128)}, f32[3072,64]{0,1:T(8,128)}, bf16[3,256,64]{1,2,0:T(8,128)(2,1)}, pred[3072]{0:T(1024)(128)(4,1)S(1)}, /...) while((s32[]{:T(128)}, f32[3072,64]{0,1:T(8,128)}, ...), condition=%wide.region_21.22_spmd.clone, body=%wide.region_17.21_spmd.clone.sunk | while | flops 516177152 | bytes 31344504 | solution.py:136
  65.4 2.7 %convolution_add_fusion.4 = f32[3072,64]{0,1:T(8,128)} fusion(f32[3072,64]{0,1:T(8,128)} %get-tuple-element.787, pred[]{:T(512)S(6)} %compare.10, bf16[3,256,64]{2,1,0:T(8,128)(2,1)} %get-tuple-element.806, s32[]{:T(128)} %get-tuple-element.785, f32[256,3072]{1,0:T(8,128)S(1)} %get-tuple-element.670, f32[256]{0:T(256)S(1)} %bitcast.189, ...), kind=kOutput, calls=%fused_computation.29.clone.1 | convolution fusion | flops 104202240 | bytes 4787713 | tf_op jit(solution)/shard_map/while/body/eval_jaxpr/dot_general | solution.py:124
  70.0 2.2 %fusion.174 = bf16[256,3072]{1,0:T(8,128)(2,1)S(1)} fusion(bf16[3072,64]{1,0:T(8,128)(2,1)} %copy-done.14, f32[256]{0:T(256)S(1)} %fusion.171, bf16[3,256,64]{2,1,0:T(8,128)(2,1)} %get-tuple-element.806, s32[]{:T(128)} %get-tuple-element.785, f32[256]{0:T(256)S(1)} %bitcast.190, f32[256]{0:T(256)S(1)} %fusion.173, ...), kind=kOutput, calls=%fused_computation.28.clone.1 | convolution fusion | flops 105381888 | bytes 5575168 | tf_op jit(solution)/shard_map/while/body/eval_jaxpr/dot_general | solution.py:109
  78.4 3.0 %convolution_add_fusion.4 = f32[3072,64]{0,1:T(8,128)} fusion(f32[3072,64]{0,1:T(8,128)} %get-tuple-element.787, pred[]{:T(512)S(6)} %compare.10, bf16[3,256,64]{2,1,0:T(8,128)(2,1)} %get-tuple-element.806, s32[]{:T(128)} %get-tuple-element.785, f32[256,3072]{1,0:T(8,128)S(1)} %get-tuple-element.670, f32[256]{0:T(256)S(1)} %bitcast.189, ...), kind=kOutput, calls=%fused_computation.29.clone.1 | convolution fusion | flops 104202240 | bytes 4787713 | tf_op jit(solution)/shard_map/while/body/eval_jaxpr/dot_general | solution.py:124
  83.3 2.2 %fusion.174 = bf16[256,3072]{1,0:T(8,128)(2,1)S(1)} fusion(bf16[3072,64]{1,0:T(8,128)(2,1)} %copy-done.14, f32[256]{0:T(256)S(1)} %fusion.171, bf16[3,256,64]{2,1,0:T(8,128)(2,1)} %get-tuple-element.806, s32[]{:T(128)} %get-tuple-element.785, f32[256]{0:T(256)S(1)} %bitcast.190, f32[256]{0:T(256)S(1)} %fusion.173, ...), kind=kOutput, calls=%fused_computation.28.clone.1 | convolution fusion | flops 105381888 | bytes 5575168 | tf_op jit(solution)/shard_map/while/body/eval_jaxpr/dot_general | solution.py:109
  85.5 2.6 %fusion.175 = f32[3072,64]{0,1:T(8,128)} fusion(bf16[256,3072]{1,0:T(8,128)(2,1)S(1)} %fusion.174, f32[3072,64]{0,1:T(8,128)} %get-tuple-element.786, pred[]{:T(512)S(6)} %compare.10, bf16[3,256,64]{2,1,0:T(8,128)(2,1)S(1)} %copy-done.8, s32[]{:T(128)} %get-tuple-element.785), kind=kOutput, calls=%fused_computation.31.clone.1 | convolution fusion | flops 101253120 | bytes 3211269 | tf_op jit(solution)/shard_map/while/body/eval_jaxpr/dot_general | solution.py:119
  93.0 3.0 %convolution_add_fusion.4 = f32[3072,64]{0,1:T(8,128)} fusion(f32[3072,64]{0,1:T(8,128)} %get-tuple-element.787, pred[]{:T(512)S(6)} %compare.10, bf16[3,256,64]{2,1,0:T(8,128)(2,1)} %get-tuple-element.806, s32[]{:T(128)} %get-tuple-element.785, f32[256,3072]{1,0:T(8,128)S(1)} %get-tuple-element.670, f32[256]{0:T(256)S(1)} %bitcast.189, ...), kind=kOutput, calls=%fused_computation.29.clone.1 | convolution fusion | flops 104202240 | bytes 4787713 | tf_op jit(solution)/shard_map/while/body/eval_jaxpr/dot_general | solution.py:124
  97.9 2.2 %fusion.174 = bf16[256,3072]{1,0:T(8,128)(2,1)S(1)} fusion(bf16[3072,64]{1,0:T(8,128)(2,1)} %copy-done.14, f32[256]{0:T(256)S(1)} %fusion.171, bf16[3,256,64]{2,1,0:T(8,128)(2,1)} %get-tuple-element.806, s32[]{:T(128)} %get-tuple-element.785, f32[256]{0:T(256)S(1)} %bitcast.190, f32[256]{0:T(256)S(1)} %fusion.173, ...), kind=kOutput, calls=%fused_computation.28.clone.1 | convolution fusion | flops 105381888 | bytes 5575168 | tf_op jit(solution)/shard_map/while/body/eval_jaxpr/dot_general | solution.py:109
  100.1 2.6 %fusion.175 = f32[3072,64]{0,1:T(8,128)} fusion(bf16[256,3072]{1,0:T(8,128)(2,1)S(1)} %fusion.174, f32[3072,64]{0,1:T(8,128)} %get-tuple-element.786, pred[]{:T(512)S(6)} %compare.10, bf16[3,256,64]{2,1,0:T(8,128)(2,1)S(1)} %copy-done.8, s32[]{:T(128)} %get-tuple-element.785), kind=kOutput, calls=%fused_computation.31.clone.1 | convolution fusion | flops 101253120 | bytes 3211269 | tf_op jit(solution)/shard_map/while/body/eval_jaxpr/dot_general | solution.py:119
  104.0 2.8 %copy.43 = f32[3072,64]{1,0:T(8,128)} copy(f32[3072,64]{0,1:T(8,128)} %get-tuple-element.202) | data formatting | bytes 1572864 | tf_op jit(solution)/shard_map/while | solution.py:136
  106.7 10.5 %while.51 = (s32[]{:T(128)}, f32[3,256,64]{1,2,0:T(8,128)S(1)}, pred[3072]{0:T(1024)(128)(4,1)S(1)}, bf16[3,256,64]{2,1,0:T(8,128)(2,1)}, bf16[3072,64]{1,0:T(8,...) while((s32[]{:T(128)}, f32[3,256,64]{1,2,0:T(8,128)S(1)}, ...), condition=%wide.region_15.16_spmd, body=%wide.region_12.15_spmd.sunk | while | flops 208403968 | bytes 12725881 | solution.py:82
  118.5 41.2 %while.53 = (s32[]{:T(128)}, f32[3072,64]{0,1:T(8,128)}, f32[3072,64]{0,1:T(8,128)}, bf16[3,256,64]{1,2,0:T(8,128)(2,1)}, pred[3072]{0:T(1024)(128)(4,1)S(1)}, /...) while((s32[]{:T(128)}, f32[3072,64]{0,1:T(8,128)}, ...), condition=%wide.region_26.27_spmd.clone, body=%wide.region_22.26_spmd.clone.sunk | while | flops 516177152 | bytes 26233576 | solution.py:136
  121.6 2.6 %convolution_add_fusion.5 = f32[3072,64]{0,1:T(8,128)} fusion(f32[3072,64]{0,1:T(8,128)} %get-tuple-element.748, pred[]{:T(512)S(6)} %compare.11, bf16[3,256,64]{2,1,0:T(8,128)(2,1)} %get-tuple-element.767, s32[]{:T(128)} %get-tuple-element.746, f32[256,3072]{1,0:T(8,128)S(1)} %get-tuple-element.683, f32[256]{0:T(256)S(1)} %bitcast.191, ...), kind=kOutput, calls=%fused_computation.61.clone.1 | convolution fusion | flops 104202240 | bytes 4787713 | tf_op jit(solution)/shard_map/while/body/eval_jaxpr/dot_general | solution.py:124
  126.1 2.1 %fusion.189 = bf16[256,3072]{1,0:T(8,128)(2,1)S(1)} fusion(bf16[3072,64]{1,0:T(8,128)(2,1)} %get-tuple-element.768, f32[256]{0:T(256)S(1)} %fusion.186, bf16[3,256,64]{2,1,0:T(8,128)(2,1)} %get-tuple-element.767, s32[]{:T(128)} %get-tuple-element.746, f32[256]{0:T(256)S(1)} %bitcast.192, f32[256]{0:T(256)S(1)} %fusion.188, ...), kind=kOutput, calls=%fused_computation.60.clone.1 | convolution fusion | flops 105381888 | bytes 5575168 | tf_op jit(solution)/shard_map/while/body/eval_jaxpr/dot_general | solution.py:109
  128.3 2.3 %fusion.190 = f32[3072,64]{0,1:T(8,128)} fusion(bf16[256,3072]{1,0:T(8,128)(2,1)S(1)} %fusion.189, f32[3072,64]{0,1:T(8,128)} %get-tuple-element.747, pred[]{:T(512)S(6)} %compare.11, bf16[3,256,64]{2,1,0:T(8,128)(2,1)} %get-tuple-element.764, s32[]{:T(128)} %get-tuple-element.746), kind=kOutput, calls=%fused_computation.63.clone.1 | convolution fusion | flops 101253120 | bytes 3211777 | tf_op jit(solution)/shard_map/while/body/eval_jaxpr/dot_general | solution.py:119
  134.9 2.9 %convolution_add_fusion.5 = f32[3072,64]{0,1:T(8,128)} fusion(f32[3072,64]{0,1:T(8,128)} %get-tuple-element.748, pred[]{:T(512)S(6)} %compare.11, bf16[3,256,64]{2,1,0:T(8,128)(2,1)} %get-tuple-element.767, s32[]{:T(128)} %get-tuple-element.746, f32[256,3072]{1,0:T(8,128)S(1)} %get-tuple-element.683, f32[256]{0:T(256)S(1)} %bitcast.191, ...), kind=kOutput, calls=%fused_computation.61.clone.1 | convolution fusion | flops 104202240 | bytes 4787713 | tf_op jit(solution)/shard_map/while/body/eval_jaxpr/dot_general | solution.py:124
  139.7 2.1 %fusion.189 = bf16[256,3072]{1,0:T(8,128)(2,1)S(1)} fusion(bf16[3072,64]{1,0:T(8,128)(2,1)} %get-tuple-element.768, f32[256]{0:T(256)S(1)} %fusion.186, bf16[3,256,64]{2,1,0:T(8,128)(2,1)} %get-tuple-element.767, s32[]{:T(128)} %get-tuple-element.746, f32[256]{0:T(256)S(1)} %bitcast.192, f32[256]{0:T(256)S(1)} %fusion.188, ...), kind=kOutput, calls=%fused_computation.60.clone.1 | convolution fusion | flops 105381888 | bytes 5575168 | tf_op jit(solution)/shard_map/while/body/eval_jaxpr/dot_general | solution.py:109
  141.9 2.6 %fusion.190 = f32[3072,64]{0,1:T(8,128)} fusion(bf16[256,3072]{1,0:T(8,128)(2,1)S(1)} %fusion.189, f32[3072,64]{0,1:T(8,128)} %get-tuple-element.747, pred[]{:T(512)S(6)} %compare.11, bf16[3,256,64]{2,1,0:T(8,128)(2,1)} %get-tuple-element.764, s32[]{:T(128)} %get-tuple-element.746), kind=kOutput, calls=%fused_computation.63.clone.1 | convolution fusion | flops 101253120 | bytes 3211777 | tf_op jit(solution)/shard_map/while/body/eval_jaxpr/dot_general | solution.py:119
  148.8 2.9 %convolution_add_fusion.5 = f32[3072,64]{0,1:T(8,128)} fusion(f32[3072,64]{0,1:T(8,128)} %get-tuple-element.748, pred[]{:T(512)S(6)} %compare.11, bf16[3,256,64]{2,1,0:T(8,128)(2,1)} %get-tuple-element.767, s32[]{:T(128)} %get-tuple-element.746, f32[256,3072]{1,0:T(8,128)S(1)} %get-tuple-element.683, f32[256]{0:T(256)S(1)} %bitcast.191, ...), kind=kOutput, calls=%fused_computation.61.clone.1 | convolution fusion | flops 104202240 | bytes 4787713 | tf_op jit(solution)/shard_map/while/body/eval_jaxpr/dot_general | solution.py:124
  153.7 2.1 %fusion.189 = bf16[256,3072]{1,0:T(8,128)(2,1)S(1)} fusion(bf16[3072,64]{1,0:T(8,128)(2,1)} %get-tuple-element.768, f32[256]{0:T(256)S(1)} %fusion.186, bf16[3,256,64]{2,1,0:T(8,128)(2,1)} %get-tuple-element.767, s32[]{:T(128)} %get-tuple-element.746, f32[256]{0:T(256)S(1)} %bitcast.192, f32[256]{0:T(256)S(1)} %fusion.188, ...), kind=kOutput, calls=%fused_computation.60.clone.1 | convolution fusion | flops 105381888 | bytes 5575168 | tf_op jit(solution)/shard_map/while/body/eval_jaxpr/dot_general | solution.py:109
  155.8 2.6 %fusion.190 = f32[3072,64]{0,1:T(8,128)} fusion(bf16[256,3072]{1,0:T(8,128)(2,1)S(1)} %fusion.189, f32[3072,64]{0,1:T(8,128)} %get-tuple-element.747, pred[]{:T(512)S(6)} %compare.11, bf16[3,256,64]{2,1,0:T(8,128)(2,1)} %get-tuple-element.764, s32[]{:T(128)} %get-tuple-element.746), kind=kOutput, calls=%fused_computation.63.clone.1 | convolution fusion | flops 101253120 | bytes 3211777 | tf_op jit(solution)/shard_map/while/body/eval_jaxpr/dot_general | solution.py:119
  164.5 2.3 %copy.47 = bf16[768,512]{0,1:T(8,128)(2,1)} copy(bf16[768,512]{1,0:T(8,128)(2,1)} %convolution_convert_fusion) | data formatting | bytes 1572864
  168.5 2.4 %collective-permute-start.9 = (bf16[768,128]{1,0:T(8,128)(2,1)}, bf16[768,128]{1,0:T(8,128)(2,1)}, u32[]{:S(2)}, u32[]{:S(2)}) collective-permute-start(bf16[768,128]{1,0:T(8,128)(2,1)} %get-tuple-element.430), channel_id=1, source_target_pairs={{0,28},{4,0},{8,4},{12,8},{16,12},{20,16},{24,20},{28,24},{1,29},{... | collective-permute-start | bytes 589832 | tf_op jit(solution)/shard_map/ppermute | solution.py:16
  170.9 2.8 %copy.41 = f32[3072,64]{1,0:T(8,128)} copy(f32[3072,64]{0,1:T(8,128)} %get-tuple-element.200) | data formatting | bytes 1572864 | tf_op jit(solution)/shard_map/while | solution.py:136
  173.7 2.8 %copy.42 = f32[3072,64]{1,0:T(8,128)} copy(f32[3072,64]{0,1:T(8,128)} %get-tuple-element.201) | data formatting | bytes 1572864 | tf_op jit(solution)/shard_map/while | solution.py:136
  176.4 2.3 %maximum_convert_fusion = bf16[3072,128]{1,0:T(8,128)(2,1)S(1)} fusion(f32[3072,64]{1,0:T(8,128)} %copy.42, f32[3072,64]{1,0:T(8,128)} %copy.41), kind=kLoop, calls=%fused_computation.88 | loop fusion | flops 1572864 | bytes 2359296 | tf_op jit(solution)/shard_map/convert.5
  188.3 3.4 %collective-permute-done.8 = bf16[768,128]{1,0:T(8,128)(2,1)S(1)} collective-permute-done((bf16[768,128]{1,0:T(8,128)(2,1)}, bf16[768,128]{1,0:T(8,128)(2,1)S(1)}, u32[]{:S(2)}, u32[]{:S(2)}) %collective-permute-start.8) | collective-permute-done | bytes 196640 | tf_op jit(solution)/shard_map/ppermute | solution.py:16
  (214 shorter events, 97.7 us)
Async XLA Ops:
  7.2 35.3 %copy-start = (bf16[128,512]{1,0:T(8,128)(2,1)S(1)}, bf16[128,512]{1,0:T(8,128)(2,1)}, u32[]{:S(2)}) copy-start(bf16[128,512]{1,0:T(8,128)(2,1)} %param.19) | copy-start | bytes 393220
  7.2 186.4 %reduce-scatter.4.cloned.1.call-start = ((), (), s32[]{:S(2)}) async-start(), calls=%async_computation.1 | async-start | bytes 983040
  7.2 39.2 %collective-permute-start = (bf16[768,128]{1,0:T(8,128)(2,1)}, bf16[768,128]{1,0:T(8,128)(2,1)S(1)}, u32[]{:S(2)}, u32[]{:S(2)}) collective-permute-start(bf16[768,128]{1,0:T(8,128)(2,1)} %param.16), channel_id=1, source_target_pairs={{0,4},{4,8},{8,12},{12,16},{16,20},{20,24},{24,28},{28,0},{1,5},{5... | collective-permute-start | bytes 589832 | tf_op jit(solution)/shard_map/ppermute | solution.py:16
  7.8 39.2 %collective-permute-start.1 = (bf16[768,128]{1,0:T(8,128)(2,1)}, bf16[768,128]{1,0:T(8,128)(2,1)S(1)}, u32[]{:S(2)}, u32[]{:S(2)}) collective-permute-start(bf16[768,128]{1,0:T(8,128)(2,1)} %param.16), channel_id=1, source_target_pairs={{0,28},{4,0},{8,4},{12,8},{16,12},{20,16},{24,20},{28,24},{1,29},{... | collective-permute-start | bytes 589832 | tf_op jit(solution)/shard_map/ppermute | solution.py:16
  10.7 36.4 %collective-permute-start.2 = (bf16[768,128]{1,0:T(8,128)(2,1)}, bf16[768,128]{1,0:T(8,128)(2,1)S(1)}, u32[]{:S(2)}, u32[]{:S(2)}) collective-permute-start(bf16[768,128]{1,0:T(8,128)(2,1)} %param.16), channel_id=1, source_target_pairs={{0,16},{4,20},{8,24},{12,28},{16,0},{20,4},{24,8},{28,12},{1,17},{... | collective-permute-start | bytes 589832 | tf_op jit(solution)/shard_map/ppermute | solution.py:16
  12.9 35.4 %collective-permute-start.3 = (bf16[768,128]{1,0:T(8,128)(2,1)}, bf16[768,128]{1,0:T(8,128)(2,1)}, u32[]{:S(2)}, u32[]{:S(2)}) collective-permute-start(bf16[768,128]{1,0:T(8,128)(2,1)} %param.17), channel_id=1, source_target_pairs={{0,4},{4,8},{8,12},{12,16},{16,20},{20,24},{24,28},{28,0},{1,5},{5... | collective-permute-start | bytes 589832 | tf_op jit(solution)/shard_map/ppermute | solution.py:16
  12.9 36.3 %collective-permute-start.4 = (bf16[768,128]{1,0:T(8,128)(2,1)}, bf16[768,128]{1,0:T(8,128)(2,1)}, u32[]{:S(2)}, u32[]{:S(2)}) collective-permute-start(bf16[768,128]{1,0:T(8,128)(2,1)} %param.17), channel_id=1, source_target_pairs={{0,28},{4,0},{8,4},{12,8},{16,12},{20,16},{24,20},{28,24},{1,29},{... | collective-permute-start | bytes 589832 | tf_op jit(solution)/shard_map/ppermute | solution.py:16
  46.4 5.9 %collective-permute-start.5 = (bf16[768,128]{1,0:T(8,128)(2,1)}, bf16[768,128]{1,0:T(8,128)(2,1)S(1)}, u32[]{:S(2)}, u32[]{:S(2)}) collective-permute-start(bf16[768,128]{1,0:T(8,128)(2,1)} %param.17), channel_id=1, source_target_pairs={{0,16},{4,20},{8,24},{12,28},{16,0},{20,4},{24,8},{28,12},{1,17},{... | collective-permute-start | bytes 589832 | tf_op jit(solution)/shard_map/ppermute | solution.py:16
  61.8 3.6 %copy-start.7 = (bf16[3,256,64]{2,1,0:T(8,128)(2,1)}, bf16[3,256,64]{2,1,0:T(8,128)(2,1)S(1)}, u32[]{:S(2)}) copy-start(bf16[3,256,64]{2,1,0:T(8,128)(2,1)S(1)} %get-tuple-element.803) | copy-start | bytes 294916 | tf_op jit(solution)/shard_map/while
  72.2 2.6 %copy-start.12 = (f32[3,256,64]{1,2,0:T(8,128)S(1)}, f32[3,256,64]{1,2,0:T(8,128)}, u32[]{:S(2)}) copy-start(f32[3,256,64]{1,2,0:T(8,128)} %copy-done.11) | copy-start | bytes 589828 | tf_op jit(solution)/shard_map/while
  72.2 2.6 %copy-start.15 = (bf16[3072,64]{1,0:T(8,128)(2,1)S(1)}, bf16[3072,64]{1,0:T(8,128)(2,1)}, u32[]{:S(2)}) copy-start(bf16[3072,64]{1,0:T(8,128)(2,1)} %copy-done.14) | copy-start | bytes 1179652 | tf_op jit(solution)/shard_map/while
  74.8 3.6 %copy-start.7 = (bf16[3,256,64]{2,1,0:T(8,128)(2,1)}, bf16[3,256,64]{2,1,0:T(8,128)(2,1)S(1)}, u32[]{:S(2)}) copy-start(bf16[3,256,64]{2,1,0:T(8,128)(2,1)S(1)} %get-tuple-element.803) | copy-start | bytes 294916 | tf_op jit(solution)/shard_map/while
  85.5 2.6 %copy-start.3 = (bf16[3072,64]{1,0:T(8,128)(2,1)S(1)}, bf16[3072,64]{1,0:T(8,128)(2,1)}, u32[]{:S(2)}) copy-start(bf16[3072,64]{1,0:T(8,128)(2,1)} %copy-done.2) | copy-start | bytes 1179652 | tf_op jit(solution)/shard_map/while
  85.5 3.9 %copy-start.12 = (f32[3,256,64]{1,2,0:T(8,128)S(1)}, f32[3,256,64]{1,2,0:T(8,128)}, u32[]{:S(2)}) copy-start(f32[3,256,64]{1,2,0:T(8,128)} %copy-done.11) | copy-start | bytes 589828 | tf_op jit(solution)/shard_map/while
  85.5 3.9 %copy-start.15 = (bf16[3072,64]{1,0:T(8,128)(2,1)S(1)}, bf16[3072,64]{1,0:T(8,128)(2,1)}, u32[]{:S(2)}) copy-start(bf16[3072,64]{1,0:T(8,128)(2,1)} %copy-done.14) | copy-start | bytes 1179652 | tf_op jit(solution)/shard_map/while
  89.4 3.6 %copy-start.7 = (bf16[3,256,64]{2,1,0:T(8,128)(2,1)}, bf16[3,256,64]{2,1,0:T(8,128)(2,1)S(1)}, u32[]{:S(2)}) copy-start(bf16[3,256,64]{2,1,0:T(8,128)(2,1)S(1)} %get-tuple-element.803) | copy-start | bytes 294916 | tf_op jit(solution)/shard_map/while
  100.1 2.6 %copy-start.3 = (bf16[3072,64]{1,0:T(8,128)(2,1)S(1)}, bf16[3072,64]{1,0:T(8,128)(2,1)}, u32[]{:S(2)}) copy-start(bf16[3072,64]{1,0:T(8,128)(2,1)} %copy-done.2) | copy-start | bytes 1179652 | tf_op jit(solution)/shard_map/while
  100.1 3.9 %copy-start.12 = (f32[3,256,64]{1,2,0:T(8,128)S(1)}, f32[3,256,64]{1,2,0:T(8,128)}, u32[]{:S(2)}) copy-start(f32[3,256,64]{1,2,0:T(8,128)} %copy-done.11) | copy-start | bytes 589828 | tf_op jit(solution)/shard_map/while
  100.1 3.9 %copy-start.15 = (bf16[3072,64]{1,0:T(8,128)(2,1)S(1)}, bf16[3072,64]{1,0:T(8,128)(2,1)}, u32[]{:S(2)}) copy-start(bf16[3072,64]{1,0:T(8,128)(2,1)} %copy-done.14) | copy-start | bytes 1179652 | tf_op jit(solution)/shard_map/while
  128.3 3.5 %copy-start.10 = (f32[3,256,64]{1,2,0:T(8,128)S(1)}, f32[3,256,64]{1,2,0:T(8,128)}, u32[]{:S(2)}) copy-start(f32[3,256,64]{1,2,0:T(8,128)} %copy-done.9) | copy-start | bytes 589828 | tf_op jit(solution)/shard_map/while
  141.9 2.6 %copy-start.1 = (bf16[3072,64]{1,0:T(8,128)(2,1)S(1)}, bf16[3072,64]{1,0:T(8,128)(2,1)}, u32[]{:S(2)}) copy-start(bf16[3072,64]{1,0:T(8,128)(2,1)} %get-tuple-element.765) | copy-start | bytes 1179652 | tf_op jit(solution)/shard_map/while
  141.9 3.8 %copy-start.10 = (f32[3,256,64]{1,2,0:T(8,128)S(1)}, f32[3,256,64]{1,2,0:T(8,128)}, u32[]{:S(2)}) copy-start(f32[3,256,64]{1,2,0:T(8,128)} %copy-done.9) | copy-start | bytes 589828 | tf_op jit(solution)/shard_map/while
  155.8 3.8 %copy-start.10 = (f32[3,256,64]{1,2,0:T(8,128)S(1)}, f32[3,256,64]{1,2,0:T(8,128)}, u32[]{:S(2)}) copy-start(f32[3,256,64]{1,2,0:T(8,128)} %copy-done.9) | copy-start | bytes 589828 | tf_op jit(solution)/shard_map/while
  159.7 7.1 %copy-start.4 = (f32[3072,64]{1,0:T(8,128)S(1)}, f32[3072,64]{1,0:T(8,128)}, u32[]{:S(2)}) copy-start(f32[3072,64]{1,0:T(8,128)} %copy.43) | copy-start | bytes 2359300
  168.0 16.7 %collective-permute-start.10 = (bf16[768,128]{1,0:T(8,128)(2,1)}, bf16[768,128]{1,0:T(8,128)(2,1)}, u32[]{:S(2)}, u32[]{:S(2)}) collective-permute-start(bf16[768,128]{1,0:T(8,128)(2,1)} %get-tuple-element.432), channel_id=1, source_target_pairs={{0,4},{4,8},{8,12},{12,16},{16,20},{20,24},{24,28},{28,0},{1,5},{5... | collective-permute-start | bytes 589832 | tf_op jit(solution)/shard_map/ppermute | solution.py:16
  168.0 18.2 %collective-permute-start.11 = (bf16[768,128]{1,0:T(8,128)(2,1)}, bf16[768,128]{1,0:T(8,128)(2,1)}, u32[]{:S(2)}, u32[]{:S(2)}) collective-permute-start(bf16[768,128]{1,0:T(8,128)(2,1)} %get-tuple-element.431), channel_id=1, source_target_pairs={{0,16},{4,20},{8,24},{12,28},{16,0},{20,4},{24,8},{28,12},{1,17},{... | collective-permute-start | bytes 589832 | tf_op jit(solution)/shard_map/ppermute | solution.py:16
  168.5 17.7 %collective-permute-start.9 = (bf16[768,128]{1,0:T(8,128)(2,1)}, bf16[768,128]{1,0:T(8,128)(2,1)}, u32[]{:S(2)}, u32[]{:S(2)}) collective-permute-start(bf16[768,128]{1,0:T(8,128)(2,1)} %get-tuple-element.430), channel_id=1, source_target_pairs={{0,28},{4,0},{8,4},{12,8},{16,12},{20,16},{24,20},{28,24},{1,29},{... | collective-permute-start | bytes 589832 | tf_op jit(solution)/shard_map/ppermute | solution.py:16
  179.5 8.8 %collective-permute-start.6 = (bf16[768,128]{1,0:T(8,128)(2,1)}, bf16[768,128]{1,0:T(8,128)(2,1)}, u32[]{:S(2)}, u32[]{:S(2)}) collective-permute-start(bf16[768,128]{1,0:T(8,128)(2,1)} %get-tuple-element.433), channel_id=1, source_target_pairs={{0,28},{4,0},{8,4},{12,8},{16,12},{20,16},{24,20},{28,24},{1,29},{... | collective-permute-start | bytes 589832 | tf_op jit(solution)/shard_map/ppermute | solution.py:16
  179.5 8.8 %collective-permute-start.7 = (bf16[768,128]{1,0:T(8,128)(2,1)}, bf16[768,128]{1,0:T(8,128)(2,1)}, u32[]{:S(2)}, u32[]{:S(2)}) collective-permute-start(bf16[768,128]{1,0:T(8,128)(2,1)} %get-tuple-element.435), channel_id=1, source_target_pairs={{0,4},{4,8},{8,12},{12,16},{16,20},{20,24},{24,28},{28,0},{1,5},{5... | collective-permute-start | bytes 589832 | tf_op jit(solution)/shard_map/ppermute | solution.py:16
  182.8 8.9 %copy-start.5 = (f32[3072,64]{1,0:T(8,128)S(1)}, f32[3072,64]{1,0:T(8,128)}, u32[]{:S(2)}) copy-start(f32[3072,64]{1,0:T(8,128)} %copy.41) | copy-start | bytes 2359300
  182.8 8.9 %copy-start.6 = (f32[3072,64]{1,0:T(8,128)S(1)}, f32[3072,64]{1,0:T(8,128)}, u32[]{:S(2)}) copy-start(f32[3072,64]{1,0:T(8,128)} %copy.42) | copy-start | bytes 2359300
  184.7 7.0 %collective-permute-start.8 = (bf16[768,128]{1,0:T(8,128)(2,1)}, bf16[768,128]{1,0:T(8,128)(2,1)S(1)}, u32[]{:S(2)}, u32[]{:S(2)}) collective-permute-start(bf16[768,128]{1,0:T(8,128)(2,1)} %get-tuple-element.434), channel_id=1, source_target_pairs={{0,16},{4,20},{8,24},{12,28},{16,0},{20,4},{24,8},{28,12},{1,17},{... | collective-permute-start | bytes 589832 | tf_op jit(solution)/shard_map/ppermute | solution.py:16
  (21 other events, 31.7 us)
Sparse Core Ops, SparseCore 0:
  166.9 21.7 reduce-scatter.3
where the time goes:
time: 204 us; the launch traced here: 202 us
  matrix products  77.4 us (38%)
  local copies, waits for them, and re-layouts  42.8 us (21%)
  other arithmetic  27 us (13%)
  blocking collectives  18.4 us (9%)
  between operations  16.3 us (8%)
  starting transfers between devices  13.9 us (7%)
  waiting for transfers between devices  5.6 us (3%)
    dot_general x12, matrix products, attention_weights(): lax.dot_general(query_rows, key_rows, (((1,), (1,)), ((), ())), preferred...  18.8 us
    all_gather x1, blocking collectives, body(): lax.all_gather(out_grad, 'head', axis=1, tiled=True)  18.4 us
    dot_general x6, matrix products, one_block(): lax.dot_general(rounded, grad_rows, (((0,), (0,)), ((), ())), preferred_e...  17.1 us
    dot_general x6, matrix products, one_block(): lax.dot_general(score_grad, query_rows, (((0,), (0,)), ((), ())), preferr...  14 us
    ppermute x12, starting transfers between devices, passed_along(): lax.ppermute(value, axis, [(i, (i + by) % size) for i in range(size)])  13.9 us
    dot_general x6, matrix products, one_block(): lax.dot_general(grad_rows, value_rows, (((1,), (1,)), ((), ())), preferre...  13 us
    while x6, local copies, waits for them, and re-layouts, head_backward(): sums, outputs = lax.scan(one_block, (zeros_start, zeros_start), inputs)  12.8 us
    unnamed x18, local copies, waits for them, and re-layouts  9.52 us
  transfers between devices with their start and end apart: 13, of which 2 were waited for; matrix products, arithmetic and copies ran while one was open for 16% of the time, Pallas kernels for 0%

commit v1 on v0

v1 whole, which is shorter than its diff:
```python
import functools
import math

import jax
import jax.numpy as jnp
from jax import lax
from jax.experimental import pallas as pl
from jax.experimental.pallas import tpu as pltpu
from jax.sharding import PartitionSpec as P

HD = 64
MASKED = -1e30
MESH = pl.DeviceIdType.MESH
F32 = jnp.float32
BF16 = jnp.bfloat16
NT = (((1,), (1,)), ((), ()))
NN = (((1,), (0,)), ((), ()))


def mm(a, b, dims=NN):
    return lax.dot_general(a, b, dims, preferred_element_type=F32)


def kernel(
    n_blk, n_head, qb,
    counts, links, q_ref, k_ref, v_ref, g_ref, w_ref,
    att_ref, dq_ref, dk_ref, dv_ref,
    kbuf, vbuf, gbuf, wbuf, fbuf, fown, kt, vt, qm, gm, gt, wts, ot, dqt, m_ref, l_ref, mslot, d_ref,
    dk_acc, dv_acc, sk, sv, rk, rv,
    kv_send, kv_recv, h_send, h_recv, r_send, r_recv,
):
    points, features = q_ref.shape
    heads = features // HD
    nq = points // qb
    scaling = 1.0 / math.sqrt(HD)
    me = lax.axis_index("blk")
    hd = lax.axis_index("head")
    half = n_blk // 2
    owners = (
        me,
        lax.rem(me + n_blk - 1, n_blk),
        lax.rem(me + 1, n_blk),
        lax.rem(me + half, n_blk),
    )
    targets = (me, owners[2], owners[1], lax.rem(me + n_blk - half, n_blk))

    barrier = pltpu.get_barrier_semaphore()
    for s in (1, 2, 3):
        pl.semaphore_signal(barrier, inc=1, device_id={"blk": owners[s]}, device_id_type=MESH)
    for r in range(1, n_head):
        pl.semaphore_signal(
            barrier, inc=1, device_id={"head": lax.rem(hd + r, n_head)}, device_id_type=MESH
        )
    pl.semaphore_wait(barrier, 3 + n_head - 1)

    def to_blk(src, dst, sends, recvs, index, target):
        return pltpu.make_async_remote_copy(
            src_ref=src, dst_ref=dst, send_sem=sends.at[index], recv_sem=recvs.at[index],
            device_id={"blk": target}, device_id_type=MESH,
        )

    def to_head(src, dst, index, target):
        return pltpu.make_async_remote_copy(
            src_ref=src, dst_ref=dst, send_sem=h_send.at[index], recv_sem=h_recv.at[index],
            device_id={"head": target}, device_id_type=MESH,
        )

    fetch = {}
    for s in (2, 1, 3):
        fetch[s] = (
            to_blk(k_ref, kbuf.at[s - 1], kv_send, kv_recv, 2 * s - 2, targets[s]),
            to_blk(v_ref, vbuf.at[s - 1], kv_send, kv_recv, 2 * s - 1, targets[s]),
        )
    gathers = []
    weights = []
    for r in range(1, n_head):
        there = lax.rem(hd + r, n_head)
        columns = pl.ds(pl.multiple_of(there * features, features), features)
        gathers.append(to_head(g_ref, gbuf.at[r - 1], r - 1, there))
        weights.append(to_head(w_ref.at[:, columns], wbuf.at[r - 1], n_head - 1 + r - 1, there))
    for s in (2, 1, 3):
        for copy in fetch[s]:
            copy.start()
    for copy in gathers + weights:
        copy.start()

    lane = lax.broadcasted_iota(jnp.int32, (1, features), 1)
    for h in range(heads):
        inside = jnp.logical_and(lane >= h * HD, lane < (h + 1) * HD)
        qm[h] = jnp.where(inside, q_ref[...].astype(F32) * scaling, 0.0).astype(BF16)
    m_ref[...] = jnp.full(m_ref.shape, MASKED, F32)
    l_ref[...] = jnp.zeros(l_ref.shape, F32)
    ot[...] = jnp.zeros(ot.shape, F32)
    dqt[...] = jnp.zeros(dqt.shape, F32)

    def forward(s, keys, values):
        kt[s] = keys[...].astype(F32).T.astype(BF16)
        vt[s] = values[...].astype(F32).T.astype(BF16)
        shown = counts[owners[s]]
        if s > 0:
            shown = shown * links[me, s - 1]
        row = lax.broadcasted_iota(jnp.int32, (points, 1), 0)
        bias = jnp.where(row < shown, 0.0, MASKED)

        for h in range(heads):

            @pl.loop(0, nq)
            def _(i):
                rows = pl.ds(pl.multiple_of(i * qb, qb), qb)
                scores = mm(keys[...], qm[h, rows, :], NT) + bias
                before = m_ref[h, i]
                top = jnp.maximum(before, jnp.max(scores, axis=0, keepdims=True))
                alpha = jnp.exp(before - top)
                powers = jnp.exp(scores - top)
                l_ref[h, i] = l_ref[h, i] * alpha + jnp.sum(powers, axis=0, keepdims=True)
                small = powers.astype(BF16)
                wts[s, h, i] = small
                ot[h, i] = ot[h, i] * alpha + mm(vt[s, h * HD:(h + 1) * HD, :], small)
                m_ref[h, i] = top
                mslot[s, h, i] = top

    forward(0, k_ref, v_ref)
    for s in (2, 1, 3):
        for copy in fetch[s]:
            copy.wait_recv()
        forward(s, kbuf.at[s - 1], vbuf.at[s - 1])

    mine = counts[me]
    for i in range(nq):
        column = lax.broadcasted_iota(jnp.int32, (1, qb), 1) + i * qb
        live = jnp.where(column < mine, 1.0, 0.0)
        for h in range(heads):
            scale = live / l_ref[h, i]
            l_ref[h, i] = scale
            ot[h, i] = ot[h, i] * scale
        fown[i * qb:(i + 1) * qb, :] = jnp.concatenate(
            [ot[h, i] for h in range(heads)], axis=0
        ).T.astype(BF16)

    for copy in gathers:
        copy.wait_recv()
    own = pl.ds(pl.multiple_of(hd * features, features), features)
    grad = mm(g_ref[...], w_ref[:, own], NT)
    for r in range(1, n_head):
        there = lax.rem(hd + n_head - r, n_head)
        columns = pl.ds(pl.multiple_of(there * features, features), features)
        grad = grad + mm(gbuf[r - 1], w_ref[:, columns], NT)
    grad = grad.astype(BF16)
    for h in range(heads):
        inside = jnp.logical_and(lane >= h * HD, lane < (h + 1) * HD)
        gm[h] = jnp.where(inside, grad.astype(F32), 0.0).astype(BF16)
    gt[...] = grad.astype(F32).T

    spread = []
    for r in range(1, n_head):
        there = lax.rem(hd + r, n_head)
        copy = to_head(fown, fbuf.at[r - 1], 2 * (n_head - 1) + r - 1, there)
        copy.start()
        spread.append(copy)

    for i in range(nq):
        for h in range(heads):
            d_ref[h, i] = jnp.sum(
                ot[h, i] * gt[h * HD:(h + 1) * HD, i * qb:(i + 1) * qb], axis=0, keepdims=True
            )

    def backward(s, values):
        for h in range(heads):

            @pl.loop(0, nq)
            def _(i):
                rows = pl.ds(pl.multiple_of(i * qb, qb), qb)
                factor = jnp.exp(mslot[s, h, i] - m_ref[h, i]) * l_ref[h, i]
                grad_rows = gm[h, rows, :]
                inner = mm(values[...], grad_rows, NT) - d_ref[h, i]
                part = wts[s, h, i].astype(F32) * factor
                score_grad = (part * inner).astype(BF16)
                value_part = mm(part.astype(BF16), grad_rows)
                key_part = mm(score_grad, qm[h, rows, :])
                dqt[h, i] += mm(kt[s, h * HD:(h + 1) * HD, :], score_grad)
                dv_acc[...] += value_part
                dk_acc[...] += key_part

    returned = []
    for s in (3, 1, 2):
        dv_acc[...] = jnp.zeros(dv_acc.shape, F32)
        dk_acc[...] = jnp.zeros(dk_acc.shape, F32)
        backward(s, vbuf.at[s - 1])
        sk[s - 1] = dk_acc[...].astype(BF16)
        sv[s - 1] = dv_acc[...].astype(BF16)
        for index, (src, dst) in enumerate(((sk, rk), (sv, rv))):
            copy = to_blk(
                src.at[s - 1], dst.at[s - 1], r_send, r_recv, 2 * s - 2 + index, owners[s]
            )
            copy.start()
            returned.append(copy)
    dv_acc[...] = jnp.zeros(dv_acc.shape, F32)
    dk_acc[...] = jnp.zeros(dk_acc.shape, F32)
    backward(0, v_ref)
    for i in range(nq):
        dq_ref[i * qb:(i + 1) * qb, :] = (
            jnp.concatenate([dqt[h, i] for h in range(heads)], axis=0).T * scaling
        ).astype(BF16)

    for copy in weights + spread:
        copy.wait_recv()
    out = mm(fown[...], w_ref[:, own])
    for r in range(1, n_head):
        out = out + mm(fbuf[r - 1], wbuf[r - 1])
    att_ref[...] = out.astype(BF16)

    for copy in returned:
        copy.wait_recv()
    dk_ref[...] = (
        dk_acc[...] + rk[0].astype(F32) + rk[1].astype(F32) + rk[2].astype(F32)
    ).astype(BF16)
    dv_ref[...] = (
        dv_acc[...] + rv[0].astype(F32) + rv[1].astype(F32) + rv[2].astype(F32)
    ).astype(BF16)

    for s in (1, 2, 3):
        for copy in fetch[s]:
            copy.wait_send()
    for copy in gathers + weights + spread + returned:
        copy.wait_send()


def body(queries, key_states, value_states, out_grad, out_weight, counts, patch_links):
    n_blk = lax.axis_size("blk")
    n_head = lax.axis_size("head")
    points, features = queries.shape
    heads = features // HD
    qb = math.gcd(points, 256)
    nq = points // qb
    rows = (points, features)
    vmem = pl.BlockSpec(memory_space=pltpu.VMEM)
    smem = pl.BlockSpec(memory_space=pltpu.SMEM)
    V = pltpu.VMEM
    dma = pltpu.SemaphoreType.DMA
    return pl.pallas_call(
        functools.partial(kernel, n_blk, n_head, qb),
        out_shape=[jax.ShapeDtypeStruct(rows, BF16)] * 4,
        in_specs=[smem, smem, vmem, vmem, vmem, vmem, vmem],
        out_specs=[vmem] * 4,
        scratch_shapes=[
            V((3,) + rows, BF16),
            V((3,) + rows, BF16),
            V((n_head - 1,) + rows, BF16),
            V((n_head - 1, features, features), BF16),
            V((n_head - 1,) + rows, BF16),
            V(rows, BF16),
            V((4, features, points), BF16),
            V((4, features, points), BF16),
            V((heads,) + rows, BF16),
            V((heads,) + rows, BF16),
            V((features, points), F32),
            V((4, heads, nq, points, qb), BF16),
            V((heads, nq, HD, qb), F32),
            V((heads, nq, HD, qb), F32),
            V((heads, nq, 1, qb), F32),
            V((heads, nq, 1, qb), F32),
            V((4, heads, nq, 1, qb), F32),
            V((heads, nq, 1, qb), F32),
            V(rows, F32),
            V(rows, F32),
            V((3,) + rows, BF16),
            V((3,) + rows, BF16),
            V((3,) + rows, BF16),
            V((3,) + rows, BF16),
            dma((6,)),
            dma((6,)),
            dma((3 * (n_head - 1),)),
            dma((3 * (n_head - 1),)),
            dma((6,)),
            dma((6,)),
        ],
        compiler_params=pltpu.CompilerParams(
            collective_id=0, has_side_effects=True, vmem_limit_bytes=56 * 1024 * 1024
        ),
    )(counts, patch_links, queries, key_states, value_states, out_grad, out_weight)


def solution(mesh):
    return jax.shard_map(
        body,
        mesh=mesh,
        in_specs=(
            P("blk", "head"),
            P("blk", "head"),
            P("blk", "head"),
            P("blk", "head"),
            P("head", None),
            P(),
            P(),
        ),
        out_specs=(P("blk", "head"), P("blk", "head"), P("blk", "head"), P("blk", "head")),
        check_vma=False,
    )
```

time: 204 us -> 54.1 us (0.27)
  matrix products: 77.4 us -> 0 us
  Pallas kernels: 0 us -> 47.6 us
  local copies, waits for them, and re-layouts: 42.8 us -> 5.68 us
  other arithmetic: 27 us -> 0 us
  blocking collectives: 18.4 us -> 0 us
  between operations: 16.3 us -> 0.65 us
  starting transfers between devices: 13.9 us -> 0 us
  waiting for transfers between devices: 5.6 us -> 0 us
    dot_general x44 -> x0, matrix products: 77.4 us -> none  [the longest x12 18.8 us: attention_weights(): lax.dot_general(query_rows, key_rows, (((1,), (1,)), ((), ())), preferred...]
    pallas_call x0 -> x1, Pallas kernels: none -> 47.6 us  [body(): pl.pallas_call(functools.partial(kernel, n_blk, n_head, qb), out_shape=[j...]
    while x78 -> x0, local copies, waits for them, and re-layouts: 18.5 us -> none  [the longest x6 12.8 us: head_backward(): sums, outputs = lax.scan(one_block, (zeros_start, zeros_start), inputs)]
    all_gather x1 -> x0, blocking collectives: 18.4 us -> none  [body(): lax.all_gather(out_grad, 'head', axis=1, tiled=True)]
    reduce_sum x19 -> x0, other arithmetic: 14.2 us -> none  [the longest x12 6.91 us: attention_weights(): total = jnp.sum(powers, axis=1, keepdims=True)]
    ppermute x12 -> x0, starting transfers between devices: 13.9 us -> none  [passed_along(): lax.ppermute(value, axis, [(i, (i + by) % size) for i in range(size)])]
    slice x6 -> x0, local copies, waits for them, and re-layouts: 5.88 us -> none  [the longest x1 1.82 us: body(): queries[:, first_column:first_column + HD]]
    dynamic_slice x24 -> x0, local copies, waits for them, and re-layouts: 5.72 us -> none  [the longest x12 5.62 us: head_backward(): sums, outputs = lax.scan(one_block, (zeros_start, zeros_start), inputs)]
  transfers between devices with their start and end apart: 13 -> 0, of which waited for: 2 -> 0; matrix products, arithmetic and copies ran while one was open for 16% -> 0% of each run, Pallas kernels for 0% -> 0%
where the time goes in v1:
time: 54.1 us; the launch traced here: 53.9 us
  Pallas kernels  47.6 us (88%)
  local copies, waits for them, and re-layouts  5.68 us (10%)
  between operations  0.65 us (1%)
    pallas_call x1, Pallas kernels, body(): pl.pallas_call(functools.partial(kernel, n_blk, n_head, qb), out_shape=[j...  47.6 us
    unnamed x11, local copies, waits for them, and re-layouts  5.68 us

profile of v1, /device:TPU:0, one launch (start us, length us, event | category | flops | bytes accessed | tf_op | source)
XLA Modules:
  0.0 53.9 jit_solution(5752148304060300237)
XLA Ops:
  0.6 1.3 %copy.11.links = s32[8,3]{1,0:T(8,128)} copy(s32[8,3]{0,1:T(4,128)} %param.13) | data formatting | bytes 192 | tf_op args[6]
  2.0 47.6 %shard_map.102 = (bf16[768,128]{1,0:T(8,128)(2,1)}, bf16[768,128]{1,0:T(8,128)(2,1)}, bf16[768,128]{1,0:T(8,128)(2,1)}, bf16[768,128]{1,0:T(8,128)(2,1)}) custom-call(s32[8]{0:T(128)} %counts.1, s32[8,3]{1,0:T(8,128)} %copy.11.links, bf16[768,128]{1,0:T(8,128)(2,1)} %q_ref.1, bf16[768,128]{1,0:T(8,128)(2,1)} %k_ref.1, bf16[768,128]{1,0:T(8,128)(2,1)} %v_ref.1, ...), custom_call_target="tpu_custom_call" | custom-call | tf_op jit(solution)/shard_map/pallas_call | solution.py:240
  49.5 0.0 copy-start.2
  49.6 1.7 %copy.16 = bf16[768,128]{1,0:T(8,128)(2,1)} copy(bf16[768,128]{1,0:T(8,128)(2,1)} %get-tuple-element.8) | data formatting | bytes 393216
  51.2 0.0 copy-done.2
  51.2 0.0 copy-start.1
  51.2 0.7 %copy.17 = bf16[768,128]{1,0:T(8,128)(2,1)} copy(bf16[768,128]{1,0:T(8,128)(2,1)S(1)} %copy-done.2) | data formatting | bytes 393216
  51.9 0.3 copy-done.1
  52.2 0.0 copy-start
  52.2 0.7 %copy.18 = bf16[768,128]{1,0:T(8,128)(2,1)} copy(bf16[768,128]{1,0:T(8,128)(2,1)S(1)} %copy-done.1) | data formatting | bytes 393216
  52.9 0.3 copy-done
  53.2 0.7 %copy.19 = bf16[768,128]{1,0:T(8,128)(2,1)} copy(bf16[768,128]{1,0:T(8,128)(2,1)S(1)} %copy-done) | data formatting | bytes 393216
Async XLA Ops:
  49.5 1.7 %copy-start.2 = (bf16[768,128]{1,0:T(8,128)(2,1)S(1)}, bf16[768,128]{1,0:T(8,128)(2,1)}, u32[]{:S(2)}) copy-start(bf16[768,128]{1,0:T(8,128)(2,1)} %get-tuple-element.9) | copy-start | bytes 589828
  51.2 1.0 %copy-start.1 = (bf16[768,128]{1,0:T(8,128)(2,1)S(1)}, bf16[768,128]{1,0:T(8,128)(2,1)}, u32[]{:S(2)}) copy-start(bf16[768,128]{1,0:T(8,128)(2,1)} %get-tuple-element.10) | copy-start | bytes 589828
  52.2 1.0 %copy-start = (bf16[768,128]{1,0:T(8,128)(2,1)S(1)}, bf16[768,128]{1,0:T(8,128)(2,1)}, u32[]{:S(2)}) copy-start(bf16[768,128]{1,0:T(8,128)(2,1)} %get-tuple-element.11) | copy-start | bytes 589828
